TPU v7x, 32 devices: a whole 2x2x4 slice. The times are simulated.
32 devices in a mesh: grp: 2 (over y), tile: 4 (over z), rep: 4 (over x, core).
Axes of the slice: x: 2, y: 2, z: 4, core: 2. Of those that a mesh axis runs over, the one named last changes fastest.
Arguments:
- focusing: bfloat16 [2, 512, 1024], P(None, 'grp', 'tile'), parts along dimension 1, may hold values from -6 to 6
- source_basis: bfloat16 [2, 64, 8, 1024], P(None, 'rep', 'grp', 'tile'), parts along dimension 2, may hold values from -0.375 to 0.375
- receiver_basis: bfloat16 [2, 64, 8, 1024], P(None, 'rep', 'grp', 'tile'), parts along dimension 2, may hold values from -0.21875 to 0.21875
- tile_ranks: int32 [8, 4], P('grp', 'tile'), parts along dimension 0, may hold values from 1 to 4
- keep_counts: int32 [8], P(('grp', 'tile')), parts along dimension 0, may hold values from 64 to 256
Outputs:
- forward_data: float32 [2, 512, 1024], P(None, ('grp', 'rep'), 'tile'), parts along dimension 1
- muted_adjoint_result: float32 [2, 512, 1024], P(None, ('grp', 'rep'), 'tile'), parts along dimension 1
- correlations: float32 [2, 256, 512], P(None, 'rep', 'grp'), parts along dimension 2
There are 2 independent parts, one for each index of `grp`. A program takes and returns all parts, laid end to end along the dimension named above; each array names one. Nothing has to cross between parts.
Inputs may be any that keep to these rules, and one draw needn't show every extreme that they name: `tile_ranks`: number of live buckets of 16 ranks in each tile. `keep_counts`: receivers kept in each receiver tile, counted from its first position.
All inputs are finite; a program needn't handle non-finite values.
Results may differ from a plain program's by a relative error of at most 0.0039.
Values may be sent and summed in bfloat16 or wider, within the bound.
No kernel may reach another device: no remote copies, remote signals or barrier semaphores. Data moves between devices by JAX's collectives and lax.ppermute only.
A program may use at most 64 MiB of HBM per device.

v0:
```python
import functools
import math

import jax
import jax.numpy as jnp
from jax import lax
from jax.experimental import pallas as pl
from jax.experimental.pallas import tpu as pltpu
from jax.sharding import PartitionSpec as P


SPAN = 256
BUCKET = 16
BF16 = jnp.bfloat16
F32 = jnp.float32

NT = (((1,), (1,)), ((), ()))
NN = (((1,), (0,)), ((), ()))
TN = (((0,), (0,)), ((), ()))


def dot(a, b, dims):
    return lax.dot_general(a, b, dims, preferred_element_type=F32)


def swap(x, step):
    count = lax.axis_size("rep")
    return lax.ppermute(x, "rep", [(i, i ^ step) for i in range(count)])


def cross(x, step, twist=0):
    reps = lax.axis_size("rep")
    count = lax.axis_size("tile") * reps
    pairs = [(i, i ^ (step * reps) ^ (twist if i % 2 else 0)) for i in range(count)]
    return lax.ppermute(x, ("tile", "rep"), pairs)


LANES = 128


def live_rows(ranks_ref, cell, shard, ranks):
    rows = lax.broadcasted_iota(jnp.int32, (ranks, 1), 0) + shard * ranks
    return rows < ranks_ref[pl.ds(cell, 1), pl.ds(0, 1)] * BUCKET


def fetch_kernel(ranks_in, *refs):
    count = (len(refs) - 3) // 2
    arrays, live_out, outs = refs[:count], refs[count], refs[count + 1 : 2 * count + 1]
    ranks_ref, sems = refs[2 * count + 1 :]
    scalars = pltpu.make_async_copy(ranks_in, ranks_ref, sems.at[count])
    copies = [pltpu.make_async_copy(ref, out, sems.at[i]) for i, (ref, out) in enumerate(zip(arrays, outs))]
    scalars.start()
    for copy in copies:
        copy.start()
    scalars.wait()
    for cell in range(ranks_in.shape[0]):
        live_out[pl.ds(cell, 1), :] = jnp.full((1, LANES), ranks_ref[cell], jnp.int32)
    for copy in copies:
        copy.wait()


def forward_kernel(ranks_ref, own_ref, pair_ref, lift_ref, foc_ref, *refs):
    ranks, tiles = own_ref.shape[1], own_ref.shape[2]
    outs, bundle, blocks = refs[:tiles], refs[tiles], refs[tiles + 1]
    here = lax.axis_index("tile")
    me = lax.axis_index("rep")
    core = lax.rem(me, 2)
    points = foc_ref.shape[0] // 2
    pieces = (own_ref, pair_ref)
    rows = [ref[part, :, cell, :] for cell in range(tiles) for ref in pieces for part in range(2)]
    prod = dot(jnp.concatenate(rows, axis=0), foc_ref[...], NT)
    for cell in range(tiles):
        for shard in range(2):
            mask = live_rows(ranks_ref, cell, me ^ shard, ranks)
            first = (cell * 2 + shard) * 2 * ranks
            real = prod[first : first + ranks]
            imag = prod[first + ranks : first + 2 * ranks]
            coef = [real[:, :points] - imag[:, points:], real[:, points:] + imag[:, :points]]
            for part in range(2):
                spot = pl.multiple_of(((core ^ shard) * 2 + part) * ranks, ranks)
                blocks[cell, pl.ds(spot, ranks), :] = jnp.where(mask, coef[part], 0.0).astype(BF16)
    for step in range(tiles):
        outs[step][...] = blocks[here ^ step]
    size = 2 * ranks
    bundle[pl.ds(0, size)] = lift_ref[...].reshape(size, tiles, points)
    bundle[pl.ds(size, size)] = own_ref[...].reshape(size, tiles, points)
    own = blocks[here, pl.ds(pl.multiple_of(core * size, size), size), :]
    bundle[pl.ds(2 * size, size // tiles)] = own.reshape(size // tiles, tiles, points)


def put_lift(out, spot, slot, real, imag):
    ranks, width = real.shape
    out[spot, slot, pl.ds(0, ranks), pl.ds(0, width)] = real
    out[spot, slot, pl.ds(0, ranks), pl.ds(width, width)] = imag
    out[spot, slot, pl.ds(ranks, ranks), pl.ds(0, width)] = -imag
    out[spot, slot, pl.ds(ranks, ranks), pl.ds(width, width)] = real


def lift_kernel(keep_ref, own_ref, pair_ref, far_ref, out, weight):
    ranks, tiles, width = own_ref.shape[1:]
    columns = lax.broadcasted_iota(jnp.int32, weight.shape, 1)
    columns = jnp.where(columns >= width, columns - width, columns)
    weight[...] = (columns < keep_ref[0]).astype(F32)
    here = lax.axis_index("tile")
    core = lax.rem(lax.axis_index("rep"), 2)
    for cell in range(tiles):
        spot = here ^ cell
        put_lift(out, spot, core, own_ref[0, :, cell, :], own_ref[1, :, cell, :])
        put_lift(out, spot, 1 - core, pair_ref[0, :, cell, :], pair_ref[1, :, cell, :])
        put_lift(out, spot, 2 + core, far_ref[pl.ds(0, ranks), cell, :], far_ref[pl.ds(ranks, ranks), cell, :])


def image_basis_kernel(ranks_ref, own_ref, pair_ref, far_ref, last_ref, out):
    ranks, tiles, width = own_ref.shape[1:]
    size = 2 * ranks
    here = lax.axis_index("tile")
    me = lax.axis_index("rep")
    core = lax.rem(me, 2)
    for cell in range(tiles):
        pieces = [(core, me, own_ref[0, :, cell, :], own_ref[1, :, cell, :])]
        pieces.append((1 - core, me ^ 1, pair_ref[0, :, cell, :], pair_ref[1, :, cell, :]))
        for slot, shard, ref in ((2 + core, me ^ 2, far_ref), (3 - core, me ^ 3, last_ref)):
            parts = [ref[pl.ds(size + part * ranks, ranks), cell, :] for part in range(2)]
            pieces.append((slot, shard, *parts))
        spot = here ^ cell
        for slot, shard, real, imag in pieces:
            mask = live_rows(ranks_ref, cell, shard, ranks)
            real = jnp.where(mask, real.astype(F32), 0.0)
            imag = jnp.where(mask, imag.astype(F32), 0.0)
            out[spot, slot, pl.ds(0, ranks), pl.ds(0, width)] = real.astype(BF16)
            out[spot, slot, pl.ds(0, ranks), pl.ds(width, width)] = (-imag).astype(BF16)
            out[spot, slot, pl.ds(ranks, ranks), pl.ds(0, width)] = imag.astype(BF16)
            out[spot, slot, pl.ds(ranks, ranks), pl.ds(width, width)] = real.astype(BF16)


def early_kernel(near_ref, far_ref, last_ref, mine_ref, lift_in, lift_ref, part_out, coef):
    tiles, reps, block, width2 = lift_ref.shape
    core = lax.rem(lax.axis_index("rep"), 2)
    here = lax.axis_index("tile")
    points = part_out.shape[0]
    ranks = block // 2
    for cell in range(tiles):
        put_lift(
            lift_ref, here ^ cell, 3 - core, last_ref[pl.ds(0, ranks), cell, :], last_ref[pl.ds(ranks, ranks), cell, :]
        )
    coef[pl.ds(0, 2)] = near_ref[...].reshape(2, block, points)
    coef[2 + core] = far_ref[pl.ds(2 * block, block // tiles)].reshape(block, points)
    coef[3 - core] = last_ref[pl.ds(2 * block, block // tiles)].reshape(block, points)
    rows = (tiles - 1) * 2 * block
    part = dot(coef[...].reshape(reps * block, points), lift_ref[0].reshape(reps * block, width2), TN)
    lift = lift_ref[pl.ds(1, tiles - 1), pl.ds(2 * core, 2)].reshape(rows, width2)
    part_out[...] = part + dot(mine_ref[...], lift, TN)


def middle_kernel(weight_ref, pair_ref, lift_ref, part_ref, *refs, factor):
    fwd_out, own_corr, own_back = refs[:3]
    tiles, reps, block, width2 = lift_ref.shape
    sends, whole = refs[3 : 2 + tiles], refs[2 + tiles]
    me = lax.axis_index("rep")
    core = lax.rem(me, 2)
    points = whole.shape[0]
    width = width2 // 2
    share = points // reps
    lift = lift_ref[pl.ds(1, tiles - 1), pl.ds(2 - 2 * core, 2)].reshape((tiles - 1) * 2 * block, width2)
    total = part_ref[...] + dot(pair_ref[...], lift, TN)
    whole[...] = total
    mine = whole[pl.ds(pl.multiple_of(me * share, share), share), :]
    fwd_out[0] = mine[:, :width]
    fwd_out[1] = mine[:, width:]
    muted = (mine * weight_ref[pl.ds(0, 1), :]).astype(BF16)
    back = dot(muted, lift_ref[...].reshape(tiles * reps * block, width2), NT).astype(BF16)
    cell = reps * block
    high = total.astype(BF16)
    low = (total - high.astype(F32)).astype(BF16)
    turned = jnp.concatenate([muted[:, width:], -muted[:, :width]], axis=1)
    left = jnp.concatenate([muted, turned], axis=0)
    corr = (dot(left, high, NT) + dot(left, low, NT)) * factor
    own_corr[...] = corr
    own_back[...] = back[:, :cell]
    small = corr.astype(BF16)
    for step in range(1, tiles):
        out = sends[step - 1]
        out[pl.ds(0, 2 * share), :] = small
        piece = back[:, step * cell : (step + 1) * cell]
        out[pl.ds(2 * share, share // 2), pl.ds(0, cell)] = piece[: share // 2]
        out[pl.ds(2 * share, share // 2), pl.ds(cell, cell)] = piece[share // 2 :]


def final_kernel(own_corr, own_back, basis_ref, *refs):
    tiles, reps, block, width2 = basis_ref.shape
    arrived = refs[: tiles - 1]
    adj_out, corr_out, adj, corr, back, sems = refs[tiles - 1 :]
    share, cell = own_back.shape
    width = width2 // 2
    half = share // 2
    for part in range(2):
        rows = pl.ds(part * share, share)
        total = own_corr[rows, :]
        for got in arrived:
            total = total + got[rows, :].astype(F32)
        corr[part] = total
    first = pltpu.make_async_copy(corr, corr_out, sems.at[0])
    first.start()
    back[:, pl.ds(0, cell)] = own_back[...]
    for step, got in enumerate(arrived, 1):
        for part in range(2):
            back[pl.ds(part * half, half), pl.ds(step * cell, cell)] = got[
                pl.ds(2 * share, half), pl.ds(part * cell, cell)
            ]
    image = dot(back[...], basis_ref[...].reshape(tiles * reps * block, width2), NN)
    adj[0] = image[:, :width]
    adj[1] = image[:, width:]
    second = pltpu.make_async_copy(adj, adj_out, sems.at[1])
    second.start()
    first.wait()
    second.wait()


def call(kernel, ins, outs, scratch, args, aliases={}):
    vmem, smem = pl.BlockSpec(memory_space=pltpu.VMEM), pl.BlockSpec(memory_space=pltpu.SMEM)
    kinds = {"s": smem, "h": pl.BlockSpec(memory_space=pl.ANY), "p": vmem}
    args = [pltpu.with_memory_space_constraint(a, pltpu.VMEM) if k == "p" else a for k, a in zip(ins, args)]
    return pl.pallas_call(
        kernel,
        in_specs=[kinds[kind] for kind in ins],
        out_specs=[vmem if isinstance(out, pl.MemoryRef) else kinds["h"] for out in outs],
        out_shape=outs,
        scratch_shapes=scratch,
        input_output_aliases=aliases,
    )(*args)


def short_path(focusing, source, receiver, tile_ranks, keep_counts):
    tiles, reps = lax.axis_size("tile"), lax.axis_size("rep")
    ranks, width = source.shape[1], source.shape[3]
    points = focusing.shape[1]
    share = points // reps
    block = 2 * ranks
    factor = 1.0 / math.sqrt(SPAN * width * tiles)
    shaped, placed = jax.ShapeDtypeStruct, pltpu.VMEM
    order = sorted(range(1, tiles), reverse=True)

    source_pair = swap(source, 1)
    receiver_pair = swap(receiver, 1)
    live, source, receiver, foc = call(
        fetch_kernel,
        "hhhh",
        [
            placed((8, LANES), jnp.int32),
            placed(source.shape, BF16),
            placed(receiver.shape, BF16),
            placed((2 * points, width), BF16),
        ],
        [pltpu.SMEM((tiles,), jnp.int32), pltpu.SemaphoreType.DMA((4,))],
        (tile_ranks.reshape(tiles), source, receiver, focusing.reshape(2 * points, width)),
    )
    made = call(
        forward_kernel,
        "ppppp",
        [placed((2 * block, points), BF16)] * tiles + [placed((2 * block + block // tiles, tiles, points), BF16)],
        [pltpu.VMEM((tiles, 2 * block, points), BF16)],
        (live, source, source_pair, receiver, foc),
    )
    far = swap(made[tiles], 2)
    got = {step: cross(made[step], step, 2) for step in order}
    last = swap(far, 1)
    gathered = jnp.concatenate([got[step] for step in range(1, tiles)], axis=0)
    spread = swap(gathered, 1)
    lift, weight = call(
        lift_kernel,
        "sppp",
        [placed((tiles, reps, block, 2 * width), BF16), placed((8, 2 * width), F32)],
        [],
        (keep_counts, receiver, receiver_pair, far),
    )
    lift, part = call(
        early_kernel,
        "ppppp",
        [placed(lift.shape, BF16), placed((points, 2 * width), F32)],
        [pltpu.VMEM((reps, block, points), BF16)],
        (made[0], far, last, gathered, lift),
        {4: 0},
    )
    middle = call(
        functools.partial(middle_kernel, factor=factor),
        "pppp",
        [placed((2, share, width), F32), placed((2 * share, points), F32), placed((share, reps * block), BF16)]
        + [placed((2 * share + share // 2, points), BF16)] * (tiles - 1),
        [pltpu.VMEM((points, 2 * width), F32)],
        (weight, spread, lift, part),
    )
    forward_data, own_corr, own_back = middle[:3]
    sent = {step: cross(middle[2 + step], step) for step in order}
    (basis,) = call(
        image_basis_kernel,
        "ppppp",
        [placed((tiles, reps, block, 2 * width), BF16)],
        [],
        (live, source, source_pair, far, last),
    )
    adjoint, corr = call(
        final_kernel,
        "p" * (tiles + 2),
        [shaped((2, share, width), F32), shaped((2, share, points), F32)],
        [
            pltpu.VMEM((2, share, width), F32),
            pltpu.VMEM((2, share, points), F32),
            pltpu.VMEM((share, tiles * reps * block), BF16),
            pltpu.SemaphoreType.DMA((2,)),
        ],
        (own_corr, own_back, basis, *[sent[step] for step in range(1, tiles)]),
    )
    return forward_data, adjoint, corr


def bucket_live(rank_column, ranks):
    return (lax.iota(jnp.int32, ranks) // BUCKET)[:, None] < rank_column[None, :]


def long_path(focusing, source_basis, receiver_basis, tile_ranks, keep_counts):
    width = focusing.shape[2]
    share = focusing.shape[1] // lax.axis_size("rep")
    weights = (lax.iota(jnp.int32, width) < keep_counts[0]).astype(F32)
    factor = 1.0 / math.sqrt(SPAN * width * lax.axis_size("tile"))
    source = lax.all_gather(source_basis, "rep", axis=1, tiled=True)
    receiver = lax.all_gather(receiver_basis, "rep", axis=1, tiled=True)
    focal = lax.dynamic_slice_in_dim(focusing, lax.axis_index("rep") * share, share, 1)
    ranks, cells = source.shape[1], source.shape[2]
    live = bucket_live(tile_ranks[:, 0], ranks)

    blocks = dot(source.reshape(-1, width), focal.reshape(-1, width), NT)
    blocks = blocks.reshape(2, ranks, cells, 2, share)
    coef = jnp.stack([blocks[0, :, :, 0] - blocks[1, :, :, 1], blocks[0, :, :, 1] + blocks[1, :, :, 0]])
    coef = jnp.where(live[None, :, :, None], coef, 0.0).astype(BF16)[:, :, :, None]
    coef = lax.all_to_all(coef, "tile", split_axis=2, concat_axis=3, tiled=True)
    coef = coef.reshape(2, ranks * cells, share)
    flat = receiver.reshape(2, ranks * cells, width)
    blocks = jnp.einsum("wgh,lgj->wlhj", coef, flat, preferred_element_type=F32)
    forward_data = jnp.stack([blocks[0, 0] - blocks[1, 1], blocks[1, 0] + blocks[0, 1]])
    masked = (forward_data * weights).astype(BF16)

    blocks = jnp.einsum("pks,qfs->pqkf", flat, masked, preferred_element_type=F32)
    back = jnp.stack([blocks[0, 0] + blocks[1, 1], blocks[0, 1] - blocks[1, 0]]).astype(BF16)
    back = back.reshape(2, ranks, 1, cells, share)
    back = lax.all_to_all(back, "tile", split_axis=3, concat_axis=2, tiled=True)
    back = jnp.where(live[None, :, :, None, None], back, jnp.zeros((), BF16)).reshape(2, ranks * cells, share)
    flat = source.reshape(2, ranks * cells, width)
    blocks = jnp.einsum("wgh,lgj->wlhj", back, flat, preferred_element_type=F32)
    adjoint = jnp.stack([blocks[0, 0] + blocks[1, 1], blocks[1, 0] - blocks[0, 1]])
    blocks = jnp.einsum(
        "pgs,qfs->pqgf", adjoint, focusing.astype(F32), precision=lax.Precision.HIGHEST, preferred_element_type=F32
    )
    corr = factor * jnp.stack([blocks[0, 0] + blocks[1, 1], blocks[1, 0] - blocks[0, 1]])
    return forward_data, adjoint, lax.psum(corr, "tile")


def solution(mesh):
    tiles, reps = mesh.shape["tile"], mesh.shape["rep"]
    short = tiles == 4 and reps == 4

    def per_device(*args):
        return (short_path if short else long_path)(*args)

    placed = (
        P(None, "grp", "tile"),
        P(None, "rep", "grp", "tile"),
        P(None, "rep", "grp", "tile"),
        P("grp", "tile"),
        P(("grp", "tile")),
    )
    return jax.shard_map(
        per_device,
        mesh=mesh,
        in_specs=placed,
        out_specs=(P(None, ("grp", "rep"), "tile"), P(None, ("grp", "rep"), "tile"), P(None, "rep", "grp")),
        check_vma=False,
    )
```

profile of v0, /device:TPU:0, one launch (start us, length us, event | category | flops | bytes accessed | tf_op | source)
XLA Modules:
  0.0 30.2 jit_solution(4915234768757805835)
XLA Ops:
  0.6 0.6 %collective-permute-start.1 = (bf16[2,16,4,256]{3,2,1,0:T(4,128)(2,1)}, bf16[2,16,4,256]{3,2,1,0:T(4,128)(2,1)S(1)}, u32[]{:S(2)}, u32[]{:S(2)}) collective-permute-start(bf16[2,16,4,256]{3,2,1,0:T(4,128)(2,1)} %refs_0_.1), channel_id=1, source_target_pairs={{0,1},{1,0},{2,3},{3,2},{4,5},{5,4},{6,7},{7,6},{8,9},{9,8},{10,11... | collective-permute-start | bytes 196616 | tf_op jit(solution)/shard_map/ppermute | solution.py:28
  1.2 1.1 %shard_map.76 = (s32[8,128]{1,0:T(8,128)S(1)}, bf16[2,16,4,256]{3,2,1,0:T(4,128)(2,1)S(1)}, bf16[2,16,4,256]{3,2,1,0:T(4,128)(2,1)S(1)}, bf16[512,256]{1,0:T(8,128)(2,1)S(1)}) custom-call(s32[4]{0:T(128)} %bitcast.3, bf16[2,16,4,256]{3,2,1,0:T(4,128)(2,1)} %refs_0_.1, bf16[2,16,4,256]{3,2,1,0:T(4,128)(2,1)} %refs_1_.1, bf16[512,256]{1,0:T(8,128)(2,1)} %bitcast.2), custom_call_target="tpu_custom_call" | custom-call | tf_op jit(solution)/shard_map/pallas_call | solution.py:223
  2.3 0.0 collective-permute-done.1.pair_ref
  2.3 0.4 %shard_map.77 = (bf16[64,256]{1,0:T(8,128)(2,1)S(1)}, bf16[64,256]{1,0:T(8,128)(2,1)S(1)}, bf16[64,256]{1,0:T(8,128)(2,1)S(1)}, bf16[64,256]{1,0:T(8,128)(2,1)S(1)}, bf16[72,4,256]{2,1,0:T(4,128)(2,1)S(1)}) custom-call(s32[8,128]{1,0:T(8,128)S(1)} %get-tuple-element.25.ranks_ref, bf16[2,16,4,256]{3,2,1,0:T(4,128)(2,1)S(1)} %get-tuple-element.26.own_ref, ...), custom_call_target="tpu_custom_call" | custom-call | tf_op jit(solution)/shard_map/pallas_call | solution.py:223
  2.7 3.0 %collective-permute-start.3 = (bf16[64,256]{1,0:T(8,128)(2,1)S(1)}, bf16[64,256]{1,0:T(8,128)(2,1)S(1)}, u32[]{:S(2)}, u32[]{:S(2)}) collective-permute-start(bf16[64,256]{1,0:T(8,128)(2,1)S(1)} %get-tuple-element.30), channel_id=1, source_target_pairs={{0,4},{1,7},{2,6},{3,5},{4,0},{5,3},{6,2},{7,1},{8,12},{9,15},{10,... | collective-permute-start | bytes 98312 | tf_op jit(solution)/shard_map/ppermute | solution.py:35
  5.7 2.6 %collective-permute-start.4 = (bf16[64,256]{1,0:T(8,128)(2,1)S(1)}, bf16[64,256]{1,0:T(8,128)(2,1)S(1)}, u32[]{:S(2)}, u32[]{:S(2)}) collective-permute-start(bf16[64,256]{1,0:T(8,128)(2,1)S(1)} %get-tuple-element.31), channel_id=1, source_target_pairs={{0,8},{1,11},{2,10},{3,9},{4,12},{5,15},{6,14},{7,13},{8,0},{9,3},... | collective-permute-start | bytes 98312 | tf_op jit(solution)/shard_map/ppermute | solution.py:35
  8.3 1.7 %collective-permute-start.2 = (bf16[72,4,256]{2,1,0:T(4,128)(2,1)S(1)}, bf16[72,4,256]{2,1,0:T(4,128)(2,1)S(1)}, u32[]{:S(2)}, u32[]{:S(2)}) collective-permute-start(bf16[72,4,256]{2,1,0:T(4,128)(2,1)S(1)} %get-tuple-element.28), channel_id=1, source_target_pairs={{0,2},{1,3},{2,0},{3,1},{4,6},{5,7},{6,4},{7,5},{8,10},{9,11},{10,... | collective-permute-start | bytes 442376 | tf_op jit(solution)/shard_map/ppermute | solution.py:28
  10.0 1.4 %collective-permute-done.4 = bf16[64,256]{1,0:T(8,128)(2,1)S(1)} collective-permute-done((bf16[64,256]{1,0:T(8,128)(2,1)S(1)}, bf16[64,256]{1,0:T(8,128)(2,1)S(1)}, u32[]{:S(2)}, u32[]{:S(2)}) %collective-permute-start.4) | collective-permute-done | bytes 32800 | tf_op jit(solution)/shard_map/ppermute | solution.py:35
  11.4 3.9 %collective-permute-done.2.far_ref = bf16[72,4,256]{2,1,0:T(4,128)(2,1)S(1)} collective-permute-done((bf16[72,4,256]{2,1,0:T(4,128)(2,1)S(1)}, bf16[72,4,256]{2,1,0:T(4,128)(2,1)S(1)}, u32[]{:S(2)}, u32[]{:S(2)}) %collective-permute-start.2) | collective-permute-done | bytes 147488 | tf_op jit(solution)/shard_map/ppermute | solution.py:28
  15.2 0.1 collective-permute-start.7
  15.4 0.4 %collective-permute-start.6 = (bf16[192,256]{1,0:T(8,128)(2,1)S(1)}, bf16[192,256]{1,0:T(8,128)(2,1)S(1)}, u32[]{:S(2)}, u32[]{:S(2)}) collective-permute-start(bf16[192,256]{1,0:T(8,128)(2,1)S(1)} %constant_dynamic-update-slice_fusion.mine_ref), channel_id=1, source_target_pairs={{0,1},{1,0},{2,3},{3,2},{4,5},{5,4},{6,7},{7,6},{8,9},{9,8},{10,11... | collective-permute-start | bytes 294920 | tf_op jit(solution)/shard_map/ppermute | solution.py:28
  15.8 0.1 collective-permute-start
  16.5 0.5 %collective-permute-done.pair_ref = bf16[2,16,4,256]{3,2,1,0:T(4,128)(2,1)S(1)} collective-permute-done((bf16[2,16,4,256]{3,2,1,0:T(4,128)(2,1)S(1)}, bf16[2,16,4,256]{3,2,1,0:T(4,128)(2,1)S(1)}, u32[]{:S(2)}, u32[]{:S(2)}) %collective-permute-start) | collective-permute-done | bytes 65568 | tf_op jit(solution)/shard_map/ppermute | solution.py:28
  17.0 0.5 %shard_map.78 = (bf16[4,4,32,512]{3,2,1,0:T(8,128)(2,1)S(1)}, f32[8,512]{1,0:T(8,128)S(1)}) custom-call(s32[1]{0:T(128)S(6)} %copy.13.keep_ref, bf16[2,16,4,256]{3,2,1,0:T(4,128)(2,1)S(1)} %get-tuple-element.24.lift_ref.own_ref, bf16[2,16,4,256]{3,2,1,0:T(4,128)(2,1)S(1)} %collective-permute-done.pair_ref, bf16[72,4,256]{2,1,0:T(4,128)(2,1)S(1)} %collective-permute-done.2.far_ref), custom_call_target="tpu_custom_call" | custom-call | tf_op jit(solution)/shard_map/pallas_call | solution.py:223
  17.6 0.5 %shard_map.79 = (bf16[4,4,32,512]{3,2,1,0:T(8,128)(2,1)S(1)}, f32[256,512]{1,0:T(8,128)S(1)}) custom-call(bf16[64,256]{1,0:T(8,128)(2,1)S(1)} %get-tuple-element.33.near_ref, bf16[72,4,256]{2,1,0:T(4,128)(2,1)S(1)} %collective-permute-done.2.far_ref, bf16[72,4,256]{2,1,0:T(4,128)(2,1)S(1)} %collective-permute-done.7.last_ref, ...), custom_call_target="tpu_custom_call", output_to_operand_aliasing={{0}: (4, {})} | custom-call | tf_op jit(solution)/shard_map/pallas_call | solution.py:223
  18.1 0.7 %shard_map.80 = (f32[2,64,256]{2,1,0:T(8,128)S(1)}, f32[128,256]{1,0:T(8,128)S(1)}, bf16[64,128]{1,0:T(8,128)(2,1)S(1)}, bf16[160,256]{1,0:T(8,128)(2,1)S(1)}, b...) custom-call(f32[8,512]{1,0:T(8,128)S(1)} %get-tuple-element.29.weight_ref, ...), custom_call_target="tpu_custom_call" | custom-call | tf_op jit(solution)/shard_map/pallas_call | solution.py:223
  18.7 3.5 %collective-permute-start.10 = (bf16[160,256]{1,0:T(8,128)(2,1)S(1)}, bf16[160,256]{1,0:T(8,128)(2,1)S(1)}, u32[]{:S(2)}, u32[]{:S(2)}) collective-permute-start(bf16[160,256]{1,0:T(8,128)(2,1)S(1)} %get-tuple-element.42), channel_id=1, source_target_pairs={{0,12},{1,13},{2,14},{3,15},{4,8},{5,9},{6,10},{7,11},{8,4},{9,5},... | collective-permute-start | bytes 245768 | tf_op jit(solution)/shard_map/ppermute | solution.py:35
  22.2 1.0 %collective-permute-start.9 = (bf16[160,256]{1,0:T(8,128)(2,1)S(1)}, bf16[160,256]{1,0:T(8,128)(2,1)S(1)}, u32[]{:S(2)}, u32[]{:S(2)}) collective-permute-start(bf16[160,256]{1,0:T(8,128)(2,1)S(1)} %get-tuple-element.41), channel_id=1, source_target_pairs={{0,8},{1,9},{2,10},{3,11},{4,12},{5,13},{6,14},{7,15},{8,0},{9,1},... | collective-permute-start | bytes 245768 | tf_op jit(solution)/shard_map/ppermute | solution.py:35
  23.2 0.7 %copy.12 = f32[2,64,256]{2,1,0:T(8,128)} copy(f32[2,64,256]{2,1,0:T(8,128)S(1)} %get-tuple-element.45) | data formatting | bytes 262144
  23.8 0.3 shard_map.81.basis_ref
  24.1 1.9 %collective-permute-done.10.refs_2_ = bf16[160,256]{1,0:T(8,128)(2,1)S(1)} collective-permute-done((bf16[160,256]{1,0:T(8,128)(2,1)S(1)}, bf16[160,256]{1,0:T(8,128)(2,1)S(1)}, u32[]{:S(2)}, u32[]{:S(2)}) %collective-permute-start.10) | collective-permute-done | bytes 81952 | tf_op jit(solution)/shard_map/ppermute | solution.py:35
  26.0 2.5 %collective-permute-done.8.refs_0_ = bf16[160,256]{1,0:T(8,128)(2,1)S(1)} collective-permute-done((bf16[160,256]{1,0:T(8,128)(2,1)S(1)}, bf16[160,256]{1,0:T(8,128)(2,1)S(1)}, u32[]{:S(2)}, u32[]{:S(2)}) %collective-permute-start.8) | collective-permute-done | bytes 81952 | tf_op jit(solution)/shard_map/ppermute | solution.py:35
  28.5 0.8 %collective-permute-done.9.refs_1_ = bf16[160,256]{1,0:T(8,128)(2,1)S(1)} collective-permute-done((bf16[160,256]{1,0:T(8,128)(2,1)S(1)}, bf16[160,256]{1,0:T(8,128)(2,1)S(1)}, u32[]{:S(2)}, u32[]{:S(2)}) %collective-permute-start.9) | collective-permute-done | bytes 81952 | tf_op jit(solution)/shard_map/ppermute | solution.py:35
  29.3 0.9 %shard_map.82 = (f32[2,64,256]{2,1,0:T(8,128)}, f32[2,64,256]{2,1,0:T(8,128)}) custom-call(f32[128,256]{1,0:T(8,128)S(1)} %get-tuple-element.38.own_corr, bf16[64,128]{1,0:T(8,128)(2,1)S(1)} %get-tuple-element.39.own_back, bf16[4,4,32,512]{3,2,1,0:T(8,128)(2,1)S(1)} %shard_map.81.basis_ref, bf16[160,256]{1,0:T(8,128)(2,1)S(1)} %collective-permute-done.8.refs_0_, ...), custom_call_target="tpu_custom_call" | custom-call | tf_op jit(solution)/shard_map/pallas_call | solution.py:223
  (11 shorter events, 0.0 us)
Async XLA Ops:
  0.6 1.7 %collective-permute-start.1 = (bf16[2,16,4,256]{3,2,1,0:T(4,128)(2,1)}, bf16[2,16,4,256]{3,2,1,0:T(4,128)(2,1)S(1)}, u32[]{:S(2)}, u32[]{:S(2)}) collective-permute-start(bf16[2,16,4,256]{3,2,1,0:T(4,128)(2,1)} %refs_0_.1), channel_id=1, source_target_pairs={{0,1},{1,0},{2,3},{3,2},{4,5},{5,4},{6,7},{7,6},{8,9},{9,8},{10,11... | collective-permute-start | bytes 196616 | tf_op jit(solution)/shard_map/ppermute | solution.py:28
  2.7 7.3 %collective-permute-start.3 = (bf16[64,256]{1,0:T(8,128)(2,1)S(1)}, bf16[64,256]{1,0:T(8,128)(2,1)S(1)}, u32[]{:S(2)}, u32[]{:S(2)}) collective-permute-start(bf16[64,256]{1,0:T(8,128)(2,1)S(1)} %get-tuple-element.30), channel_id=1, source_target_pairs={{0,4},{1,7},{2,6},{3,5},{4,0},{5,3},{6,2},{7,1},{8,12},{9,15},{10,... | collective-permute-start | bytes 98312 | tf_op jit(solution)/shard_map/ppermute | solution.py:35
  5.7 5.7 %collective-permute-start.4 = (bf16[64,256]{1,0:T(8,128)(2,1)S(1)}, bf16[64,256]{1,0:T(8,128)(2,1)S(1)}, u32[]{:S(2)}, u32[]{:S(2)}) collective-permute-start(bf16[64,256]{1,0:T(8,128)(2,1)S(1)} %get-tuple-element.31), channel_id=1, source_target_pairs={{0,8},{1,11},{2,10},{3,9},{4,12},{5,15},{6,14},{7,13},{8,0},{9,3},... | collective-permute-start | bytes 98312 | tf_op jit(solution)/shard_map/ppermute | solution.py:35
  8.3 7.1 %collective-permute-start.5 = (bf16[64,256]{1,0:T(8,128)(2,1)S(1)}, bf16[64,256]{1,0:T(8,128)(2,1)S(1)}, u32[]{:S(2)}, u32[]{:S(2)}) collective-permute-start(bf16[64,256]{1,0:T(8,128)(2,1)S(1)} %get-tuple-element.32), channel_id=1, source_target_pairs={{0,12},{1,15},{2,14},{3,13},{4,8},{5,11},{6,10},{7,9},{8,4},{9,7},... | collective-permute-start | bytes 98312 | tf_op jit(solution)/shard_map/ppermute | solution.py:35
  8.3 7.0 %collective-permute-start.2 = (bf16[72,4,256]{2,1,0:T(4,128)(2,1)S(1)}, bf16[72,4,256]{2,1,0:T(4,128)(2,1)S(1)}, u32[]{:S(2)}, u32[]{:S(2)}) collective-permute-start(bf16[72,4,256]{2,1,0:T(4,128)(2,1)S(1)} %get-tuple-element.28), channel_id=1, source_target_pairs={{0,2},{1,3},{2,0},{3,1},{4,6},{5,7},{6,4},{7,5},{8,10},{9,11},{10,... | collective-permute-start | bytes 442376 | tf_op jit(solution)/shard_map/ppermute | solution.py:28
  10.0 5.8 %copy-start = (bf16[2,16,4,256]{3,2,1,0:T(4,128)(2,1)S(1)}, bf16[2,16,4,256]{3,2,1,0:T(4,128)(2,1)}, u32[]{:S(2)}) copy-start(bf16[2,16,4,256]{3,2,1,0:T(4,128)(2,1)} %refs_1_.1) | copy-start | bytes 196612
  15.2 2.3 %collective-permute-start.7 = (bf16[72,4,256]{2,1,0:T(4,128)(2,1)S(1)}, bf16[72,4,256]{2,1,0:T(4,128)(2,1)S(1)}, u32[]{:S(2)}, u32[]{:S(2)}) collective-permute-start(bf16[72,4,256]{2,1,0:T(4,128)(2,1)S(1)} %collective-permute-done.2.far_ref), channel_id=1, source_target_pairs={{0,1},{1,0},{2,3},{3,2},{4,5},{5,4},{6,7},{7,6},{8,9},{9,8},{10,11... | collective-permute-start | bytes 442376 | tf_op jit(solution)/shard_map/ppermute | solution.py:28
  15.4 2.7 %collective-permute-start.6 = (bf16[192,256]{1,0:T(8,128)(2,1)S(1)}, bf16[192,256]{1,0:T(8,128)(2,1)S(1)}, u32[]{:S(2)}, u32[]{:S(2)}) collective-permute-start(bf16[192,256]{1,0:T(8,128)(2,1)S(1)} %constant_dynamic-update-slice_fusion.mine_ref), channel_id=1, source_target_pairs={{0,1},{1,0},{2,3},{3,2},{4,5},{5,4},{6,7},{7,6},{8,9},{9,8},{10,11... | collective-permute-start | bytes 294920 | tf_op jit(solution)/shard_map/ppermute | solution.py:28
  15.8 1.3 %collective-permute-start = (bf16[2,16,4,256]{3,2,1,0:T(4,128)(2,1)S(1)}, bf16[2,16,4,256]{3,2,1,0:T(4,128)(2,1)S(1)}, u32[]{:S(2)}, u32[]{:S(2)}) collective-permute-start(bf16[2,16,4,256]{3,2,1,0:T(4,128)(2,1)S(1)} %copy-done), channel_id=1, source_target_pairs={{0,1},{1,0},{2,3},{3,2},{4,5},{5,4},{6,7},{7,6},{8,9},{9,8},{10,11... | collective-permute-start | bytes 196616 | tf_op jit(solution)/shard_map/ppermute | solution.py:28
  18.7 7.3 %collective-permute-start.10 = (bf16[160,256]{1,0:T(8,128)(2,1)S(1)}, bf16[160,256]{1,0:T(8,128)(2,1)S(1)}, u32[]{:S(2)}, u32[]{:S(2)}) collective-permute-start(bf16[160,256]{1,0:T(8,128)(2,1)S(1)} %get-tuple-element.42), channel_id=1, source_target_pairs={{0,12},{1,13},{2,14},{3,15},{4,8},{5,9},{6,10},{7,11},{8,4},{9,5},... | collective-permute-start | bytes 245768 | tf_op jit(solution)/shard_map/ppermute | solution.py:35
  22.2 6.3 %collective-permute-start.8 = (bf16[160,256]{1,0:T(8,128)(2,1)S(1)}, bf16[160,256]{1,0:T(8,128)(2,1)S(1)}, u32[]{:S(2)}, u32[]{:S(2)}) collective-permute-start(bf16[160,256]{1,0:T(8,128)(2,1)S(1)} %get-tuple-element.40), channel_id=1, source_target_pairs={{0,4},{1,5},{2,6},{3,7},{4,0},{5,1},{6,2},{7,3},{8,12},{9,13},{10,... | collective-permute-start | bytes 245768 | tf_op jit(solution)/shard_map/ppermute | solution.py:35
  22.2 7.1 %collective-permute-start.9 = (bf16[160,256]{1,0:T(8,128)(2,1)S(1)}, bf16[160,256]{1,0:T(8,128)(2,1)S(1)}, u32[]{:S(2)}, u32[]{:S(2)}) collective-permute-start(bf16[160,256]{1,0:T(8,128)(2,1)S(1)} %get-tuple-element.41), channel_id=1, source_target_pairs={{0,8},{1,9},{2,10},{3,11},{4,12},{5,13},{6,14},{7,15},{8,0},{9,1},... | collective-permute-start | bytes 245768 | tf_op jit(solution)/shard_map/ppermute | solution.py:35
where the time goes:
time: 30.4 us; the launch traced here: 30.2 us
  starting transfers between devices  12.9 us (42%)
  waiting for transfers between devices  11 us (36%)
  Pallas kernels  4.3 us (14%)
  between operations  1.35 us (4%)
  local copies, waits for them, and re-layouts  0.67 us (2%)
    ppermute x6, starting transfers between devices, cross(): return lax.ppermute(x, ('tile', 'rep'), pairs)  10 us
    ppermute x6, waiting for transfers between devices, cross(): return lax.ppermute(x, ('tile', 'rep'), pairs)  6.54 us
    ppermute x5, waiting for transfers between devices, swap(): return lax.ppermute(x, 'rep', [(i, i ^ step) for i in range(count)])  4.42 us
    pallas_call x7, Pallas kernels, call(): pl.pallas_call(kernel, in_specs=[kinds[kind] for kind in ins], out_specs=...  4.3 us
    ppermute x5, starting transfers between devices, swap(): return lax.ppermute(x, 'rep', [(i, i ^ step) for i in range(count)])  2.89 us
    unnamed x5, local copies, waits for them, and re-layouts  0.66 us
  transfers between devices with their start and end apart: 11, of which 6 were waited for; matrix products, arithmetic and copies ran while one was open for 2% of the time, Pallas kernels for 8%

commit v1 on v0

--- a/solution.py
+++ b/solution.py
@@ -155,7 +155,7 @@
 def middle_kernel(weight_ref, pair_ref, lift_ref, part_ref, *refs, factor):
     fwd_out, own_corr, own_back = refs[:3]
     tiles, reps, block, width2 = lift_ref.shape
-    sends, whole = refs[3 : 2 + tiles], refs[2 + tiles]
+    sends, whole, high = refs[3 : 2 + tiles], refs[2 + tiles], refs[3 + tiles]
     me = lax.axis_index("rep")
     core = lax.rem(me, 2)
     points = whole.shape[0]
@@ -163,54 +163,79 @@
     share = points // reps
     lift = lift_ref[pl.ds(1, tiles - 1), pl.ds(2 - 2 * core, 2)].reshape((tiles - 1) * 2 * block, width2)
     total = part_ref[...] + dot(pair_ref[...], lift, TN)
+    small = total.astype(BF16)
     whole[...] = total
-    mine = whole[pl.ds(pl.multiple_of(me * share, share), share), :]
+    high[pl.ds(0, points), :] = small
+    high[pl.ds(points, points), :] = small
+    first = pl.multiple_of(me * share, share)
+    mine = whole[pl.ds(first, share), :]
     fwd_out[0] = mine[:, :width]
     fwd_out[1] = mine[:, width:]
     muted = (mine * weight_ref[pl.ds(0, 1), :]).astype(BF16)
     back = dot(muted, lift_ref[...].reshape(tiles * reps * block, width2), NT).astype(BF16)
     cell = reps * block
-    high = total.astype(BF16)
-    low = (total - high.astype(F32)).astype(BF16)
     turned = jnp.concatenate([muted[:, width:], -muted[:, :width]], axis=1)
     left = jnp.concatenate([muted, turned], axis=0)
-    corr = (dot(left, high, NT) + dot(left, low, NT)) * factor
+    corr = dot(left, high[pl.ds(first, points), :], NT) * factor
     own_corr[...] = corr
     own_back[...] = back[:, :cell]
-    small = corr.astype(BF16)
+    mixed = (corr[:share, :share] + corr[share:, :share]).astype(BF16)
+    rest = corr.astype(BF16)
+    group = share * (cell - share) // points
     for step in range(1, tiles):
         out = sends[step - 1]
-        out[pl.ds(0, 2 * share), :] = small
         piece = back[:, step * cell : (step + 1) * cell]
-        out[pl.ds(2 * share, share // 2), pl.ds(0, cell)] = piece[: share // 2]
-        out[pl.ds(2 * share, share // 2), pl.ds(cell, cell)] = piece[share // 2 :]
-
-
-def final_kernel(own_corr, own_back, basis_ref, *refs):
-    tiles, reps, block, width2 = basis_ref.shape
-    arrived = refs[: tiles - 1]
-    adj_out, corr_out, adj, corr, back, sems = refs[tiles - 1 :]
+        out[pl.ds(0, 2 * share), :] = rest
+        out[pl.ds(0, share), pl.ds(0, share)] = mixed
+        out[pl.ds(share, share), pl.ds(0, share)] = piece[:, :share]
+        for part in range(share // group):
+            rows = piece[part * group : (part + 1) * group, share:]
+            out[pl.ds(2 * share, group), pl.ds(part * share, share)] = rows
+
+
+def unpacked(got, out):
+    share, cell = out.shape
+    group = share * (cell - share) // got.shape[1]
+    out[:, pl.ds(0, share)] = got[pl.ds(share, share), pl.ds(0, share)]
+    for part in range(share // group):
+        rows = got[pl.ds(2 * share, group), pl.ds(part * share, share)]
+        out[pl.ds(part * group, group), pl.ds(share, cell - share)] = rows
+
+
+def sum_kernel(own_back, basis_ref, *refs):
+    tiles, _, _, width2 = basis_ref.shape
+    arrived, (image_out, corr_out, back) = refs[: tiles - 2], refs[tiles - 2 :]
     share, cell = own_back.shape
+    image = dot(own_back[...], basis_ref[0].reshape(cell, width2), NN)
+    for step, got in enumerate(arrived, 1):
+        unpacked(got, back)
+        image += dot(back[...], basis_ref[step].reshape(cell, width2), NN)
+    image_out[...] = image
+    corr_out[...] = sum(got[pl.ds(0, 2 * share), :].astype(F32) for got in arrived)
+
+
+def final_kernel(own_corr, corr_ref, image_ref, basis_ref, got, adj_out, corr_out, adj, corr, back, sems):
+    tiles, _, _, width2 = basis_ref.shape
+    share, cell = back.shape
+    points = own_corr.shape[1]
     width = width2 // 2
-    half = share // 2
-    for part in range(2):
-        rows = pl.ds(part * share, share)
-        total = own_corr[rows, :]
-        for got in arrived:
-            total = total + got[rows, :].astype(F32)
-        corr[part] = total
-    first = pltpu.make_async_copy(corr, corr_out, sems.at[0])
-    first.start()
-    back[:, pl.ds(0, cell)] = own_back[...]
-    for step, got in enumerate(arrived, 1):
-        for part in range(2):
-            back[pl.ds(part * half, half), pl.ds(step * cell, cell)] = got[
-                pl.ds(2 * share, half), pl.ds(part * cell, cell)
-            ]
-    image = dot(back[...], basis_ref[...].reshape(tiles * reps * block, width2), NN)
+    unpacked(got, back)
+    image = image_ref[...] + dot(back[...], basis_ref[tiles - 1].reshape(cell, width2), NN)
     adj[0] = image[:, :width]
     adj[1] = image[:, width:]
-    second = pltpu.make_async_copy(adj, adj_out, sems.at[1])
+    first = pltpu.make_async_copy(adj, adj_out, sems.at[0])
+    first.start()
+    arrived = corr_ref[...] + got[pl.ds(0, 2 * share), :].astype(F32)
+    mixed = arrived[:share, :share] * 0.5
+    turned = mixed.T
+    shift = lax.axis_index("rep") * share
+    lanes = lax.broadcasted_iota(jnp.int32, (share, points), 1)
+    for part, block_sum in enumerate((mixed + turned, mixed - turned)):
+        rows = slice(part * share, (part + 1) * share)
+        padded = jnp.concatenate([block_sum, jnp.zeros((share, points - share), F32)], axis=1)
+        total = own_corr[rows, :] + jnp.where(lanes < share, padded, arrived[rows])
+        corr[part] = pltpu.roll(total, shift, 1)
+    second = pltpu.make_async_copy(corr, corr_out, sems.at[1])
     second.start()
     first.wait()
     second.wait()
@@ -285,8 +310,8 @@
         functools.partial(middle_kernel, factor=factor),
         "pppp",
         [placed((2, share, width), F32), placed((2 * share, points), F32), placed((share, reps * block), BF16)]
-        + [placed((2 * share + share // 2, points), BF16)] * (tiles - 1),
-        [pltpu.VMEM((points, 2 * width), F32)],
+        + [placed((2 * share + share * (reps * block - share) // points, points), BF16)] * (tiles - 1),
+        [pltpu.VMEM((points, 2 * width), F32), pltpu.VMEM((2 * points, 2 * width), BF16)],
         (weight, spread, lift, part),
     )
     forward_data, own_corr, own_back = middle[:3]
@@ -298,17 +323,24 @@
         [],
         (live, source, source_pair, far, last),
     )
+    image_part, corr_part = call(
+        sum_kernel,
+        "p" * tiles,
+        [placed((share, 2 * width), F32), placed((2 * share, points), F32)],
+        [pltpu.VMEM((share, reps * block), BF16)],
+        (own_back, basis, *[sent[step] for step in range(1, tiles - 1)]),
+    )
     adjoint, corr = call(
         final_kernel,
-        "p" * (tiles + 2),
+        "ppppp",
         [shaped((2, share, width), F32), shaped((2, share, points), F32)],
         [
             pltpu.VMEM((2, share, width), F32),
             pltpu.VMEM((2, share, points), F32),
-            pltpu.VMEM((share, tiles * reps * block), BF16),
+            pltpu.VMEM((share, reps * block), BF16),
             pltpu.SemaphoreType.DMA((2,)),
         ],
-        (own_corr, own_back, basis, *[sent[step] for step in range(1, tiles)]),
+        (own_corr, corr_part, image_part, basis, sent[tiles - 1]),
     )
     return forward_data, adjoint, corr
 

time: 30.4 us -> 30.1 us (level)
  waiting for transfers between devices: 11 us -> 10.4 us
    ppermute x6, waiting for transfers between devices: 6.54 us -> 5.99 us  [cross(): return lax.ppermute(x, ('tile', 'rep'), pairs)]
    pallas_call x7 -> x8, Pallas kernels: 4.3 us -> 4.58 us  [call(): pl.pallas_call(kernel, in_specs=[kinds[kind] for kind in ins], out_specs=...]
  transfers between devices with their start and end apart: 11 -> 11, of which waited for: 6 -> 5; matrix products, arithmetic and copies ran while one was open for 2% -> 2% of each run, Pallas kernels for 8% -> 9%
where the time goes in v1:
time: 30.1 us; the launch traced here: 29.9 us
  starting transfers between devices  12.9 us (43%)
  waiting for transfers between devices  10.4 us (35%)
  Pallas kernels  4.58 us (15%)
  between operations  1.35 us (4%)
  local copies, waits for them, and re-layouts  0.67 us (2%)
    ppermute x6, starting transfers between devices, cross(): return lax.ppermute(x, ('tile', 'rep'), pairs)  10 us
    ppermute x6, waiting for transfers between devices, cross(): return lax.ppermute(x, ('tile', 'rep'), pairs)  5.99 us
    pallas_call x8, Pallas kernels, call(): pl.pallas_call(kernel, in_specs=[kinds[kind] for kind in ins], out_specs=...  4.58 us
    ppermute x5, waiting for transfers between devices, swap(): return lax.ppermute(x, 'rep', [(i, i ^ step) for i in range(count)])  4.42 us
    ppermute x5, starting transfers between devices, swap(): return lax.ppermute(x, 'rep', [(i, i ^ step) for i in range(count)])  2.89 us
    unnamed x5, local copies, waits for them, and re-layouts  0.66 us
  transfers between devices with their start and end apart: 11, of which 5 were waited for; matrix products, arithmetic and copies ran while one was open for 2% of the time, Pallas kernels for 9%

profile of v1, /device:TPU:0, one launch (start us, length us, event | category | flops | bytes accessed | tf_op | source)
XLA Modules:
  0.0 29.9 jit_solution(9760020398889640300)
XLA Ops:
  0.6 0.6 %collective-permute-start.1 = (bf16[2,16,4,256]{3,2,1,0:T(4,128)(2,1)}, bf16[2,16,4,256]{3,2,1,0:T(4,128)(2,1)S(1)}, u32[]{:S(2)}, u32[]{:S(2)}) collective-permute-start(bf16[2,16,4,256]{3,2,1,0:T(4,128)(2,1)} %refs_0_.1), channel_id=1, source_target_pairs={{0,1},{1,0},{2,3},{3,2},{4,5},{5,4},{6,7},{7,6},{8,9},{9,8},{10,11... | collective-permute-start | bytes 196616 | tf_op jit(solution)/shard_map/ppermute | solution.py:28
  1.2 1.1 %shard_map.76 = (s32[8,128]{1,0:T(8,128)S(1)}, bf16[2,16,4,256]{3,2,1,0:T(4,128)(2,1)S(1)}, bf16[2,16,4,256]{3,2,1,0:T(4,128)(2,1)S(1)}, bf16[512,256]{1,0:T(8,128)(2,1)S(1)}) custom-call(s32[4]{0:T(128)} %bitcast.3, bf16[2,16,4,256]{3,2,1,0:T(4,128)(2,1)} %refs_0_.1, bf16[2,16,4,256]{3,2,1,0:T(4,128)(2,1)} %refs_1_.1, bf16[512,256]{1,0:T(8,128)(2,1)} %bitcast.2), custom_call_target="tpu_custom_call" | custom-call | tf_op jit(solution)/shard_map/pallas_call | solution.py:248
  2.3 0.4 %shard_map.77 = (bf16[64,256]{1,0:T(8,128)(2,1)S(1)}, bf16[64,256]{1,0:T(8,128)(2,1)S(1)}, bf16[64,256]{1,0:T(8,128)(2,1)S(1)}, bf16[64,256]{1,0:T(8,128)(2,1)S(1)}, bf16[72,4,256]{2,1,0:T(4,128)(2,1)S(1)}) custom-call(s32[8,128]{1,0:T(8,128)S(1)} %get-tuple-element.27.ranks_ref, bf16[2,16,4,256]{3,2,1,0:T(4,128)(2,1)S(1)} %get-tuple-element.28.own_ref, ...), custom_call_target="tpu_custom_call" | custom-call | tf_op jit(solution)/shard_map/pallas_call | solution.py:248
  2.7 3.0 %collective-permute-start.3 = (bf16[64,256]{1,0:T(8,128)(2,1)S(1)}, bf16[64,256]{1,0:T(8,128)(2,1)S(1)}, u32[]{:S(2)}, u32[]{:S(2)}) collective-permute-start(bf16[64,256]{1,0:T(8,128)(2,1)S(1)} %get-tuple-element.32), channel_id=1, source_target_pairs={{0,4},{1,7},{2,6},{3,5},{4,0},{5,3},{6,2},{7,1},{8,12},{9,15},{10,... | collective-permute-start | bytes 98312 | tf_op jit(solution)/shard_map/ppermute | solution.py:35
  5.7 2.6 %collective-permute-start.4 = (bf16[64,256]{1,0:T(8,128)(2,1)S(1)}, bf16[64,256]{1,0:T(8,128)(2,1)S(1)}, u32[]{:S(2)}, u32[]{:S(2)}) collective-permute-start(bf16[64,256]{1,0:T(8,128)(2,1)S(1)} %get-tuple-element.33), channel_id=1, source_target_pairs={{0,8},{1,11},{2,10},{3,9},{4,12},{5,15},{6,14},{7,13},{8,0},{9,3},... | collective-permute-start | bytes 98312 | tf_op jit(solution)/shard_map/ppermute | solution.py:35
  8.3 1.7 %collective-permute-start.2 = (bf16[72,4,256]{2,1,0:T(4,128)(2,1)S(1)}, bf16[72,4,256]{2,1,0:T(4,128)(2,1)S(1)}, u32[]{:S(2)}, u32[]{:S(2)}) collective-permute-start(bf16[72,4,256]{2,1,0:T(4,128)(2,1)S(1)} %get-tuple-element.30), channel_id=1, source_target_pairs={{0,2},{1,3},{2,0},{3,1},{4,6},{5,7},{6,4},{7,5},{8,10},{9,11},{10,... | collective-permute-start | bytes 442376 | tf_op jit(solution)/shard_map/ppermute | solution.py:28
  10.0 1.4 %collective-permute-done.4 = bf16[64,256]{1,0:T(8,128)(2,1)S(1)} collective-permute-done((bf16[64,256]{1,0:T(8,128)(2,1)S(1)}, bf16[64,256]{1,0:T(8,128)(2,1)S(1)}, u32[]{:S(2)}, u32[]{:S(2)}) %collective-permute-start.4) | collective-permute-done | bytes 32800 | tf_op jit(solution)/shard_map/ppermute | solution.py:35
  11.4 3.9 %collective-permute-done.2.far_ref = bf16[72,4,256]{2,1,0:T(4,128)(2,1)S(1)} collective-permute-done((bf16[72,4,256]{2,1,0:T(4,128)(2,1)S(1)}, bf16[72,4,256]{2,1,0:T(4,128)(2,1)S(1)}, u32[]{:S(2)}, u32[]{:S(2)}) %collective-permute-start.2) | collective-permute-done | bytes 147488 | tf_op jit(solution)/shard_map/ppermute | solution.py:28
  15.2 0.1 collective-permute-start.7
  15.4 0.4 %collective-permute-start.6 = (bf16[192,256]{1,0:T(8,128)(2,1)S(1)}, bf16[192,256]{1,0:T(8,128)(2,1)S(1)}, u32[]{:S(2)}, u32[]{:S(2)}) collective-permute-start(bf16[192,256]{1,0:T(8,128)(2,1)S(1)} %constant_dynamic-update-slice_fusion.mine_ref), channel_id=1, source_target_pairs={{0,1},{1,0},{2,3},{3,2},{4,5},{5,4},{6,7},{7,6},{8,9},{9,8},{10,11... | collective-permute-start | bytes 294920 | tf_op jit(solution)/shard_map/ppermute | solution.py:28
  15.8 0.1 collective-permute-start
  16.5 0.5 %collective-permute-done.pair_ref = bf16[2,16,4,256]{3,2,1,0:T(4,128)(2,1)S(1)} collective-permute-done((bf16[2,16,4,256]{3,2,1,0:T(4,128)(2,1)S(1)}, bf16[2,16,4,256]{3,2,1,0:T(4,128)(2,1)S(1)}, u32[]{:S(2)}, u32[]{:S(2)}) %collective-permute-start) | collective-permute-done | bytes 65568 | tf_op jit(solution)/shard_map/ppermute | solution.py:28
  17.0 0.5 %shard_map.78 = (bf16[4,4,32,512]{3,2,1,0:T(8,128)(2,1)S(1)}, f32[8,512]{1,0:T(8,128)S(1)}) custom-call(s32[1]{0:T(128)S(6)} %copy.13.keep_ref, bf16[2,16,4,256]{3,2,1,0:T(4,128)(2,1)S(1)} %get-tuple-element.26.lift_ref.own_ref, bf16[2,16,4,256]{3,2,1,0:T(4,128)(2,1)S(1)} %collective-permute-done.pair_ref, bf16[72,4,256]{2,1,0:T(4,128)(2,1)S(1)} %collective-permute-done.2.far_ref), custom_call_target="tpu_custom_call" | custom-call | tf_op jit(solution)/shard_map/pallas_call | solution.py:248
  17.6 0.5 %shard_map.79 = (bf16[4,4,32,512]{3,2,1,0:T(8,128)(2,1)S(1)}, f32[256,512]{1,0:T(8,128)S(1)}) custom-call(bf16[64,256]{1,0:T(8,128)(2,1)S(1)} %get-tuple-element.35.near_ref, bf16[72,4,256]{2,1,0:T(4,128)(2,1)S(1)} %collective-permute-done.2.far_ref, bf16[72,4,256]{2,1,0:T(4,128)(2,1)S(1)} %collective-permute-done.7.last_ref, ...), custom_call_target="tpu_custom_call", output_to_operand_aliasing={{0}: (4, {})} | custom-call | tf_op jit(solution)/shard_map/pallas_call | solution.py:248
  18.1 0.6 %shard_map.80 = (f32[2,64,256]{2,1,0:T(8,128)S(1)}, f32[128,256]{1,0:T(8,128)S(1)}, bf16[64,128]{1,0:T(8,128)(2,1)S(1)}, bf16[144,256]{1,0:T(8,128)(2,1)S(1)}, b...) custom-call(f32[8,512]{1,0:T(8,128)S(1)} %get-tuple-element.31.weight_ref, ...), custom_call_target="tpu_custom_call" | custom-call | tf_op jit(solution)/shard_map/pallas_call | solution.py:248
  18.7 0.9 %collective-permute-start.8 = (bf16[144,256]{1,0:T(8,128)(2,1)S(1)}, bf16[144,256]{1,0:T(8,128)(2,1)S(1)}, u32[]{:S(2)}, u32[]{:S(2)}) collective-permute-start(bf16[144,256]{1,0:T(8,128)(2,1)S(1)} %get-tuple-element.42), channel_id=1, source_target_pairs={{0,4},{1,5},{2,6},{3,7},{4,0},{5,1},{6,2},{7,3},{8,12},{9,13},{10,... | collective-permute-start | bytes 221192 | tf_op jit(solution)/shard_map/ppermute | solution.py:35
  19.6 3.1 %collective-permute-start.9 = (bf16[144,256]{1,0:T(8,128)(2,1)S(1)}, bf16[144,256]{1,0:T(8,128)(2,1)S(1)}, u32[]{:S(2)}, u32[]{:S(2)}) collective-permute-start(bf16[144,256]{1,0:T(8,128)(2,1)S(1)} %get-tuple-element.43), channel_id=1, source_target_pairs={{0,8},{1,9},{2,10},{3,11},{4,12},{5,13},{6,14},{7,15},{8,0},{9,1},... | collective-permute-start | bytes 221192 | tf_op jit(solution)/shard_map/ppermute | solution.py:35
  22.7 0.4 %collective-permute-start.10 = (bf16[144,256]{1,0:T(8,128)(2,1)S(1)}, bf16[144,256]{1,0:T(8,128)(2,1)S(1)}, u32[]{:S(2)}, u32[]{:S(2)}) collective-permute-start(bf16[144,256]{1,0:T(8,128)(2,1)S(1)} %get-tuple-element.46), channel_id=1, source_target_pairs={{0,12},{1,13},{2,14},{3,15},{4,8},{5,9},{6,10},{7,11},{8,4},{9,5},... | collective-permute-start | bytes 221192 | tf_op jit(solution)/shard_map/ppermute | solution.py:35
  23.1 0.7 %copy.12 = f32[2,64,256]{2,1,0:T(8,128)} copy(f32[2,64,256]{2,1,0:T(8,128)S(1)} %get-tuple-element.49) | data formatting | bytes 262144
  23.8 0.3 shard_map.81.basis_ref
  24.1 3.9 %collective-permute-done.9.refs_1_ = bf16[144,256]{1,0:T(8,128)(2,1)S(1)} collective-permute-done((bf16[144,256]{1,0:T(8,128)(2,1)S(1)}, bf16[144,256]{1,0:T(8,128)(2,1)S(1)}, u32[]{:S(2)}, u32[]{:S(2)}) %collective-permute-start.9) | collective-permute-done | bytes 73760 | tf_op jit(solution)/shard_map/ppermute | solution.py:35
  28.0 0.3 shard_map.82
  28.2 0.8 %collective-permute-done.10.got = bf16[144,256]{1,0:T(8,128)(2,1)S(1)} collective-permute-done((bf16[144,256]{1,0:T(8,128)(2,1)S(1)}, bf16[144,256]{1,0:T(8,128)(2,1)S(1)}, u32[]{:S(2)}, u32[]{:S(2)}) %collective-permute-start.10) | collective-permute-done | bytes 73760 | tf_op jit(solution)/shard_map/ppermute | solution.py:35
  29.0 0.9 %shard_map.83 = (f32[2,64,256]{2,1,0:T(8,128)}, f32[2,64,256]{2,1,0:T(8,128)}) custom-call(f32[128,256]{1,0:T(8,128)S(1)} %get-tuple-element.40.own_corr, f32[128,256]{1,0:T(8,128)S(1)} %get-tuple-element.44.corr_ref, f32[64,512]{1,0:T(8,128)S(1)} %get-tuple-element.45.image_ref, bf16[4,4,32,512]{3,2,1,0:T(8,128)(2,1)S(1)} %shard_map.81.basis_ref, ...), custom_call_target="tpu_custom_call" | custom-call | tf_op jit(solution)/shard_map/pallas_call | solution.py:248
  (12 shorter events, 0.1 us)
Async XLA Ops:
  0.6 1.7 %collective-permute-start.1 = (bf16[2,16,4,256]{3,2,1,0:T(4,128)(2,1)}, bf16[2,16,4,256]{3,2,1,0:T(4,128)(2,1)S(1)}, u32[]{:S(2)}, u32[]{:S(2)}) collective-permute-start(bf16[2,16,4,256]{3,2,1,0:T(4,128)(2,1)} %refs_0_.1), channel_id=1, source_target_pairs={{0,1},{1,0},{2,3},{3,2},{4,5},{5,4},{6,7},{7,6},{8,9},{9,8},{10,11... | collective-permute-start | bytes 196616 | tf_op jit(solution)/shard_map/ppermute | solution.py:28
  2.7 7.3 %collective-permute-start.3 = (bf16[64,256]{1,0:T(8,128)(2,1)S(1)}, bf16[64,256]{1,0:T(8,128)(2,1)S(1)}, u32[]{:S(2)}, u32[]{:S(2)}) collective-permute-start(bf16[64,256]{1,0:T(8,128)(2,1)S(1)} %get-tuple-element.32), channel_id=1, source_target_pairs={{0,4},{1,7},{2,6},{3,5},{4,0},{5,3},{6,2},{7,1},{8,12},{9,15},{10,... | collective-permute-start | bytes 98312 | tf_op jit(solution)/shard_map/ppermute | solution.py:35
  5.7 5.7 %collective-permute-start.4 = (bf16[64,256]{1,0:T(8,128)(2,1)S(1)}, bf16[64,256]{1,0:T(8,128)(2,1)S(1)}, u32[]{:S(2)}, u32[]{:S(2)}) collective-permute-start(bf16[64,256]{1,0:T(8,128)(2,1)S(1)} %get-tuple-element.33), channel_id=1, source_target_pairs={{0,8},{1,11},{2,10},{3,9},{4,12},{5,15},{6,14},{7,13},{8,0},{9,3},... | collective-permute-start | bytes 98312 | tf_op jit(solution)/shard_map/ppermute | solution.py:35
  8.3 7.1 %collective-permute-start.5 = (bf16[64,256]{1,0:T(8,128)(2,1)S(1)}, bf16[64,256]{1,0:T(8,128)(2,1)S(1)}, u32[]{:S(2)}, u32[]{:S(2)}) collective-permute-start(bf16[64,256]{1,0:T(8,128)(2,1)S(1)} %get-tuple-element.34), channel_id=1, source_target_pairs={{0,12},{1,15},{2,14},{3,13},{4,8},{5,11},{6,10},{7,9},{8,4},{9,7},... | collective-permute-start | bytes 98312 | tf_op jit(solution)/shard_map/ppermute | solution.py:35
  8.3 7.0 %collective-permute-start.2 = (bf16[72,4,256]{2,1,0:T(4,128)(2,1)S(1)}, bf16[72,4,256]{2,1,0:T(4,128)(2,1)S(1)}, u32[]{:S(2)}, u32[]{:S(2)}) collective-permute-start(bf16[72,4,256]{2,1,0:T(4,128)(2,1)S(1)} %get-tuple-element.30), channel_id=1, source_target_pairs={{0,2},{1,3},{2,0},{3,1},{4,6},{5,7},{6,4},{7,5},{8,10},{9,11},{10,... | collective-permute-start | bytes 442376 | tf_op jit(solution)/shard_map/ppermute | solution.py:28
  10.0 5.8 %copy-start = (bf16[2,16,4,256]{3,2,1,0:T(4,128)(2,1)S(1)}, bf16[2,16,4,256]{3,2,1,0:T(4,128)(2,1)}, u32[]{:S(2)}) copy-start(bf16[2,16,4,256]{3,2,1,0:T(4,128)(2,1)} %refs_1_.1) | copy-start | bytes 196612
  15.2 2.3 %collective-permute-start.7 = (bf16[72,4,256]{2,1,0:T(4,128)(2,1)S(1)}, bf16[72,4,256]{2,1,0:T(4,128)(2,1)S(1)}, u32[]{:S(2)}, u32[]{:S(2)}) collective-permute-start(bf16[72,4,256]{2,1,0:T(4,128)(2,1)S(1)} %collective-permute-done.2.far_ref), channel_id=1, source_target_pairs={{0,1},{1,0},{2,3},{3,2},{4,5},{5,4},{6,7},{7,6},{8,9},{9,8},{10,11... | collective-permute-start | bytes 442376 | tf_op jit(solution)/shard_map/ppermute | solution.py:28
  15.4 2.7 %collective-permute-start.6 = (bf16[192,256]{1,0:T(8,128)(2,1)S(1)}, bf16[192,256]{1,0:T(8,128)(2,1)S(1)}, u32[]{:S(2)}, u32[]{:S(2)}) collective-permute-start(bf16[192,256]{1,0:T(8,128)(2,1)S(1)} %constant_dynamic-update-slice_fusion.mine_ref), channel_id=1, source_target_pairs={{0,1},{1,0},{2,3},{3,2},{4,5},{5,4},{6,7},{7,6},{8,9},{9,8},{10,11... | collective-permute-start | bytes 294920 | tf_op jit(solution)/shard_map/ppermute | solution.py:28
  15.8 1.3 %collective-permute-start = (bf16[2,16,4,256]{3,2,1,0:T(4,128)(2,1)S(1)}, bf16[2,16,4,256]{3,2,1,0:T(4,128)(2,1)S(1)}, u32[]{:S(2)}, u32[]{:S(2)}) collective-permute-start(bf16[2,16,4,256]{3,2,1,0:T(4,128)(2,1)S(1)} %copy-done), channel_id=1, source_target_pairs={{0,1},{1,0},{2,3},{3,2},{4,5},{5,4},{6,7},{7,6},{8,9},{9,8},{10,11... | collective-permute-start | bytes 196616 | tf_op jit(solution)/shard_map/ppermute | solution.py:28
  18.7 5.4 %collective-permute-start.8 = (bf16[144,256]{1,0:T(8,128)(2,1)S(1)}, bf16[144,256]{1,0:T(8,128)(2,1)S(1)}, u32[]{:S(2)}, u32[]{:S(2)}) collective-permute-start(bf16[144,256]{1,0:T(8,128)(2,1)S(1)} %get-tuple-element.42), channel_id=1, source_target_pairs={{0,4},{1,5},{2,6},{3,7},{4,0},{5,1},{6,2},{7,3},{8,12},{9,13},{10,... | collective-permute-start | bytes 221192 | tf_op jit(solution)/shard_map/ppermute | solution.py:35
  19.6 8.3 %collective-permute-start.9 = (bf16[144,256]{1,0:T(8,128)(2,1)S(1)}, bf16[144,256]{1,0:T(8,128)(2,1)S(1)}, u32[]{:S(2)}, u32[]{:S(2)}) collective-permute-start(bf16[144,256]{1,0:T(8,128)(2,1)S(1)} %get-tuple-element.43), channel_id=1, source_target_pairs={{0,8},{1,9},{2,10},{3,11},{4,12},{5,13},{6,14},{7,15},{8,0},{9,1},... | collective-permute-start | bytes 221192 | tf_op jit(solution)/shard_map/ppermute | solution.py:35
  22.7 6.3 %collective-permute-start.10 = (bf16[144,256]{1,0:T(8,128)(2,1)S(1)}, bf16[144,256]{1,0:T(8,128)(2,1)S(1)}, u32[]{:S(2)}, u32[]{:S(2)}) collective-permute-start(bf16[144,256]{1,0:T(8,128)(2,1)S(1)} %get-tuple-element.46), channel_id=1, source_target_pairs={{0,12},{1,13},{2,14},{3,15},{4,8},{5,9},{6,10},{7,11},{8,4},{9,5},... | collective-permute-start | bytes 221192 | tf_op jit(solution)/shard_map/ppermute | solution.py:35

commit v2 on v0

--- a/solution.py
+++ b/solution.py
@@ -155,7 +155,7 @@
 def middle_kernel(weight_ref, pair_ref, lift_ref, part_ref, *refs, factor):
     fwd_out, own_corr, own_back = refs[:3]
     tiles, reps, block, width2 = lift_ref.shape
-    sends, whole = refs[3 : 2 + tiles], refs[2 + tiles]
+    sends, whole, high = refs[3 : 2 + tiles], refs[2 + tiles], refs[3 + tiles]
     me = lax.axis_index("rep")
     core = lax.rem(me, 2)
     points = whole.shape[0]
@@ -163,27 +163,34 @@
     share = points // reps
     lift = lift_ref[pl.ds(1, tiles - 1), pl.ds(2 - 2 * core, 2)].reshape((tiles - 1) * 2 * block, width2)
     total = part_ref[...] + dot(pair_ref[...], lift, TN)
+    small = total.astype(BF16)
     whole[...] = total
-    mine = whole[pl.ds(pl.multiple_of(me * share, share), share), :]
+    high[pl.ds(0, points), :] = small
+    high[pl.ds(points, points), :] = small
+    first = pl.multiple_of(me * share, share)
+    mine = whole[pl.ds(first, share), :]
     fwd_out[0] = mine[:, :width]
     fwd_out[1] = mine[:, width:]
     muted = (mine * weight_ref[pl.ds(0, 1), :]).astype(BF16)
     back = dot(muted, lift_ref[...].reshape(tiles * reps * block, width2), NT).astype(BF16)
     cell = reps * block
-    high = total.astype(BF16)
-    low = (total - high.astype(F32)).astype(BF16)
     turned = jnp.concatenate([muted[:, width:], -muted[:, :width]], axis=1)
     left = jnp.concatenate([muted, turned], axis=0)
-    corr = (dot(left, high, NT) + dot(left, low, NT)) * factor
+    corr = dot(left, high[pl.ds(first, points), :], NT) * factor
     own_corr[...] = corr
     own_back[...] = back[:, :cell]
-    small = corr.astype(BF16)
+    mixed = (corr[:share, :share] + corr[share:, :share]).astype(BF16)
+    rest = corr.astype(BF16)
+    group = share * (cell - share) // points
     for step in range(1, tiles):
         out = sends[step - 1]
-        out[pl.ds(0, 2 * share), :] = small
         piece = back[:, step * cell : (step + 1) * cell]
-        out[pl.ds(2 * share, share // 2), pl.ds(0, cell)] = piece[: share // 2]
-        out[pl.ds(2 * share, share // 2), pl.ds(cell, cell)] = piece[share // 2 :]
+        out[pl.ds(0, 2 * share), :] = rest
+        out[pl.ds(0, share), pl.ds(0, share)] = mixed
+        out[pl.ds(share, share), pl.ds(0, share)] = piece[:, :share]
+        for part in range(share // group):
+            rows = piece[part * group : (part + 1) * group, share:]
+            out[pl.ds(2 * share, group), pl.ds(part * share, share)] = rows
 
 
 def final_kernel(own_corr, own_back, basis_ref, *refs):
@@ -191,27 +198,32 @@
     arrived = refs[: tiles - 1]
     adj_out, corr_out, adj, corr, back, sems = refs[tiles - 1 :]
     share, cell = own_back.shape
+    points = own_corr.shape[1]
     width = width2 // 2
-    half = share // 2
-    for part in range(2):
+    group = share * (cell - share) // points
+    mixed = sum(got[pl.ds(0, share), pl.ds(0, share)].astype(F32) for got in arrived) * 0.5
+    turned = mixed.T
+    shift = lax.axis_index("rep") * share
+    lanes = lax.broadcasted_iota(jnp.int32, (share, points), 1)
+    for part, block_sum in enumerate((mixed + turned, mixed - turned)):
         rows = pl.ds(part * share, share)
-        total = own_corr[rows, :]
-        for got in arrived:
-            total = total + got[rows, :].astype(F32)
-        corr[part] = total
-    first = pltpu.make_async_copy(corr, corr_out, sems.at[0])
-    first.start()
+        others = sum(got[rows, :].astype(F32) for got in arrived)
+        padded = jnp.concatenate([block_sum, jnp.zeros((share, points - share), F32)], axis=1)
+        total = own_corr[rows, :] + jnp.where(lanes < share, padded, others)
+        corr[part] = pltpu.roll(total, shift, 1)
+    second = pltpu.make_async_copy(corr, corr_out, sems.at[1])
+    second.start()
     back[:, pl.ds(0, cell)] = own_back[...]
     for step, got in enumerate(arrived, 1):
-        for part in range(2):
-            back[pl.ds(part * half, half), pl.ds(step * cell, cell)] = got[
-                pl.ds(2 * share, half), pl.ds(part * cell, cell)
-            ]
+        back[:, pl.ds(step * cell, share)] = got[pl.ds(share, share), pl.ds(0, share)]
+        for part in range(share // group):
+            rows = got[pl.ds(2 * share, group), pl.ds(part * share, share)]
+            back[pl.ds(part * group, group), pl.ds(step * cell + share, cell - share)] = rows
     image = dot(back[...], basis_ref[...].reshape(tiles * reps * block, width2), NN)
     adj[0] = image[:, :width]
     adj[1] = image[:, width:]
-    second = pltpu.make_async_copy(adj, adj_out, sems.at[1])
-    second.start()
+    first = pltpu.make_async_copy(adj, adj_out, sems.at[0])
+    first.start()
     first.wait()
     second.wait()
 
@@ -285,8 +297,8 @@
         functools.partial(middle_kernel, factor=factor),
         "pppp",
         [placed((2, share, width), F32), placed((2 * share, points), F32), placed((share, reps * block), BF16)]
-        + [placed((2 * share + share // 2, points), BF16)] * (tiles - 1),
-        [pltpu.VMEM((points, 2 * width), F32)],
+        + [placed((2 * share + share * (reps * block - share) // points, points), BF16)] * (tiles - 1),
+        [pltpu.VMEM((points, 2 * width), F32), pltpu.VMEM((2 * points, 2 * width), BF16)],
         (weight, spread, lift, part),
     )
     forward_data, own_corr, own_back = middle[:3]

time: 30.4 us -> 30.1 us (level)
  no operation moved by 1% of the time
where the time goes in v2:
time: 30.1 us; the launch traced here: 29.9 us
  starting transfers between devices  12.9 us (43%)
  waiting for transfers between devices  10.7 us (36%)
  Pallas kernels  4.33 us (14%)
  between operations  1.34 us (4%)
  local copies, waits for them, and re-layouts  0.67 us (2%)
    ppermute x6, starting transfers between devices, cross(): return lax.ppermute(x, ('tile', 'rep'), pairs)  10 us
    ppermute x6, waiting for transfers between devices, cross(): return lax.ppermute(x, ('tile', 'rep'), pairs)  6.27 us
    ppermute x5, waiting for transfers between devices, swap(): return lax.ppermute(x, 'rep', [(i, i ^ step) for i in range(count)])  4.42 us
    pallas_call x7, Pallas kernels, call(): pl.pallas_call(kernel, in_specs=[kinds[kind] for kind in ins], out_specs=...  4.33 us
    ppermute x5, starting transfers between devices, swap(): return lax.ppermute(x, 'rep', [(i, i ^ step) for i in range(count)])  2.89 us
    unnamed x5, local copies, waits for them, and re-layouts  0.66 us
  transfers between devices with their start and end apart: 11, of which 6 were waited for; matrix products, arithmetic and copies ran while one was open for 2% of the time, Pallas kernels for 8%

profile of v2, /device:TPU:0, one launch (start us, length us, event | category | flops | bytes accessed | tf_op | source)
XLA Modules:
  0.0 29.9 jit_solution(15080163238171450195)
XLA Ops:
  0.6 0.6 %collective-permute-start.1 = (bf16[2,16,4,256]{3,2,1,0:T(4,128)(2,1)}, bf16[2,16,4,256]{3,2,1,0:T(4,128)(2,1)S(1)}, u32[]{:S(2)}, u32[]{:S(2)}) collective-permute-start(bf16[2,16,4,256]{3,2,1,0:T(4,128)(2,1)} %refs_0_.1), channel_id=1, source_target_pairs={{0,1},{1,0},{2,3},{3,2},{4,5},{5,4},{6,7},{7,6},{8,9},{9,8},{10,11... | collective-permute-start | bytes 196616 | tf_op jit(solution)/shard_map/ppermute | solution.py:28
  1.2 1.1 %shard_map.76 = (s32[8,128]{1,0:T(8,128)S(1)}, bf16[2,16,4,256]{3,2,1,0:T(4,128)(2,1)S(1)}, bf16[2,16,4,256]{3,2,1,0:T(4,128)(2,1)S(1)}, bf16[512,256]{1,0:T(8,128)(2,1)S(1)}) custom-call(s32[4]{0:T(128)} %bitcast.3, bf16[2,16,4,256]{3,2,1,0:T(4,128)(2,1)} %refs_0_.1, bf16[2,16,4,256]{3,2,1,0:T(4,128)(2,1)} %refs_1_.1, bf16[512,256]{1,0:T(8,128)(2,1)} %bitcast.2), custom_call_target="tpu_custom_call" | custom-call | tf_op jit(solution)/shard_map/pallas_call | solution.py:235
  2.3 0.0 collective-permute-done.1.pair_ref
  2.3 0.4 %shard_map.77 = (bf16[64,256]{1,0:T(8,128)(2,1)S(1)}, bf16[64,256]{1,0:T(8,128)(2,1)S(1)}, bf16[64,256]{1,0:T(8,128)(2,1)S(1)}, bf16[64,256]{1,0:T(8,128)(2,1)S(1)}, bf16[72,4,256]{2,1,0:T(4,128)(2,1)S(1)}) custom-call(s32[8,128]{1,0:T(8,128)S(1)} %get-tuple-element.25.ranks_ref, bf16[2,16,4,256]{3,2,1,0:T(4,128)(2,1)S(1)} %get-tuple-element.26.own_ref, ...), custom_call_target="tpu_custom_call" | custom-call | tf_op jit(solution)/shard_map/pallas_call | solution.py:235
  2.7 3.0 %collective-permute-start.3 = (bf16[64,256]{1,0:T(8,128)(2,1)S(1)}, bf16[64,256]{1,0:T(8,128)(2,1)S(1)}, u32[]{:S(2)}, u32[]{:S(2)}) collective-permute-start(bf16[64,256]{1,0:T(8,128)(2,1)S(1)} %get-tuple-element.30), channel_id=1, source_target_pairs={{0,4},{1,7},{2,6},{3,5},{4,0},{5,3},{6,2},{7,1},{8,12},{9,15},{10,... | collective-permute-start | bytes 98312 | tf_op jit(solution)/shard_map/ppermute | solution.py:35
  5.7 2.6 %collective-permute-start.4 = (bf16[64,256]{1,0:T(8,128)(2,1)S(1)}, bf16[64,256]{1,0:T(8,128)(2,1)S(1)}, u32[]{:S(2)}, u32[]{:S(2)}) collective-permute-start(bf16[64,256]{1,0:T(8,128)(2,1)S(1)} %get-tuple-element.31), channel_id=1, source_target_pairs={{0,8},{1,11},{2,10},{3,9},{4,12},{5,15},{6,14},{7,13},{8,0},{9,3},... | collective-permute-start | bytes 98312 | tf_op jit(solution)/shard_map/ppermute | solution.py:35
  8.3 1.7 %collective-permute-start.2 = (bf16[72,4,256]{2,1,0:T(4,128)(2,1)S(1)}, bf16[72,4,256]{2,1,0:T(4,128)(2,1)S(1)}, u32[]{:S(2)}, u32[]{:S(2)}) collective-permute-start(bf16[72,4,256]{2,1,0:T(4,128)(2,1)S(1)} %get-tuple-element.28), channel_id=1, source_target_pairs={{0,2},{1,3},{2,0},{3,1},{4,6},{5,7},{6,4},{7,5},{8,10},{9,11},{10,... | collective-permute-start | bytes 442376 | tf_op jit(solution)/shard_map/ppermute | solution.py:28
  10.0 1.4 %collective-permute-done.4 = bf16[64,256]{1,0:T(8,128)(2,1)S(1)} collective-permute-done((bf16[64,256]{1,0:T(8,128)(2,1)S(1)}, bf16[64,256]{1,0:T(8,128)(2,1)S(1)}, u32[]{:S(2)}, u32[]{:S(2)}) %collective-permute-start.4) | collective-permute-done | bytes 32800 | tf_op jit(solution)/shard_map/ppermute | solution.py:35
  11.4 3.9 %collective-permute-done.2.far_ref = bf16[72,4,256]{2,1,0:T(4,128)(2,1)S(1)} collective-permute-done((bf16[72,4,256]{2,1,0:T(4,128)(2,1)S(1)}, bf16[72,4,256]{2,1,0:T(4,128)(2,1)S(1)}, u32[]{:S(2)}, u32[]{:S(2)}) %collective-permute-start.2) | collective-permute-done | bytes 147488 | tf_op jit(solution)/shard_map/ppermute | solution.py:28
  15.2 0.1 collective-permute-start.7
  15.4 0.4 %collective-permute-start.6 = (bf16[192,256]{1,0:T(8,128)(2,1)S(1)}, bf16[192,256]{1,0:T(8,128)(2,1)S(1)}, u32[]{:S(2)}, u32[]{:S(2)}) collective-permute-start(bf16[192,256]{1,0:T(8,128)(2,1)S(1)} %constant_dynamic-update-slice_fusion.mine_ref), channel_id=1, source_target_pairs={{0,1},{1,0},{2,3},{3,2},{4,5},{5,4},{6,7},{7,6},{8,9},{9,8},{10,11... | collective-permute-start | bytes 294920 | tf_op jit(solution)/shard_map/ppermute | solution.py:28
  15.8 0.1 collective-permute-start
  16.5 0.5 %collective-permute-done.pair_ref = bf16[2,16,4,256]{3,2,1,0:T(4,128)(2,1)S(1)} collective-permute-done((bf16[2,16,4,256]{3,2,1,0:T(4,128)(2,1)S(1)}, bf16[2,16,4,256]{3,2,1,0:T(4,128)(2,1)S(1)}, u32[]{:S(2)}, u32[]{:S(2)}) %collective-permute-start) | collective-permute-done | bytes 65568 | tf_op jit(solution)/shard_map/ppermute | solution.py:28
  17.0 0.5 %shard_map.78 = (bf16[4,4,32,512]{3,2,1,0:T(8,128)(2,1)S(1)}, f32[8,512]{1,0:T(8,128)S(1)}) custom-call(s32[1]{0:T(128)S(6)} %copy.13.keep_ref, bf16[2,16,4,256]{3,2,1,0:T(4,128)(2,1)S(1)} %get-tuple-element.24.lift_ref.own_ref, bf16[2,16,4,256]{3,2,1,0:T(4,128)(2,1)S(1)} %collective-permute-done.pair_ref, bf16[72,4,256]{2,1,0:T(4,128)(2,1)S(1)} %collective-permute-done.2.far_ref), custom_call_target="tpu_custom_call" | custom-call | tf_op jit(solution)/shard_map/pallas_call | solution.py:235
  17.6 0.5 %shard_map.79 = (bf16[4,4,32,512]{3,2,1,0:T(8,128)(2,1)S(1)}, f32[256,512]{1,0:T(8,128)S(1)}) custom-call(bf16[64,256]{1,0:T(8,128)(2,1)S(1)} %get-tuple-element.33.near_ref, bf16[72,4,256]{2,1,0:T(4,128)(2,1)S(1)} %collective-permute-done.2.far_ref, bf16[72,4,256]{2,1,0:T(4,128)(2,1)S(1)} %collective-permute-done.7.last_ref, ...), custom_call_target="tpu_custom_call", output_to_operand_aliasing={{0}: (4, {})} | custom-call | tf_op jit(solution)/shard_map/pallas_call | solution.py:235
  18.1 0.6 %shard_map.80 = (f32[2,64,256]{2,1,0:T(8,128)S(1)}, f32[128,256]{1,0:T(8,128)S(1)}, bf16[64,128]{1,0:T(8,128)(2,1)S(1)}, bf16[144,256]{1,0:T(8,128)(2,1)S(1)}, b...) custom-call(f32[8,512]{1,0:T(8,128)S(1)} %get-tuple-element.29.weight_ref, ...), custom_call_target="tpu_custom_call" | custom-call | tf_op jit(solution)/shard_map/pallas_call | solution.py:235
  18.7 3.5 %collective-permute-start.10 = (bf16[144,256]{1,0:T(8,128)(2,1)S(1)}, bf16[144,256]{1,0:T(8,128)(2,1)S(1)}, u32[]{:S(2)}, u32[]{:S(2)}) collective-permute-start(bf16[144,256]{1,0:T(8,128)(2,1)S(1)} %get-tuple-element.42), channel_id=1, source_target_pairs={{0,12},{1,13},{2,14},{3,15},{4,8},{5,9},{6,10},{7,11},{8,4},{9,5},... | collective-permute-start | bytes 221192 | tf_op jit(solution)/shard_map/ppermute | solution.py:35
  22.2 1.0 %collective-permute-start.9 = (bf16[144,256]{1,0:T(8,128)(2,1)S(1)}, bf16[144,256]{1,0:T(8,128)(2,1)S(1)}, u32[]{:S(2)}, u32[]{:S(2)}) collective-permute-start(bf16[144,256]{1,0:T(8,128)(2,1)S(1)} %get-tuple-element.41), channel_id=1, source_target_pairs={{0,8},{1,9},{2,10},{3,11},{4,12},{5,13},{6,14},{7,15},{8,0},{9,1},... | collective-permute-start | bytes 221192 | tf_op jit(solution)/shard_map/ppermute | solution.py:35
  23.1 0.7 %copy.12 = f32[2,64,256]{2,1,0:T(8,128)} copy(f32[2,64,256]{2,1,0:T(8,128)S(1)} %get-tuple-element.45) | data formatting | bytes 262144
  23.8 0.3 shard_map.81.basis_ref
  24.1 1.7 %collective-permute-done.10.refs_2_ = bf16[144,256]{1,0:T(8,128)(2,1)S(1)} collective-permute-done((bf16[144,256]{1,0:T(8,128)(2,1)S(1)}, bf16[144,256]{1,0:T(8,128)(2,1)S(1)}, u32[]{:S(2)}, u32[]{:S(2)}) %collective-permute-start.10) | collective-permute-done | bytes 73760 | tf_op jit(solution)/shard_map/ppermute | solution.py:35
  25.8 2.5 %collective-permute-done.8.refs_0_ = bf16[144,256]{1,0:T(8,128)(2,1)S(1)} collective-permute-done((bf16[144,256]{1,0:T(8,128)(2,1)S(1)}, bf16[144,256]{1,0:T(8,128)(2,1)S(1)}, u32[]{:S(2)}, u32[]{:S(2)}) %collective-permute-start.8) | collective-permute-done | bytes 73760 | tf_op jit(solution)/shard_map/ppermute | solution.py:35
  28.3 0.7 %collective-permute-done.9.refs_1_ = bf16[144,256]{1,0:T(8,128)(2,1)S(1)} collective-permute-done((bf16[144,256]{1,0:T(8,128)(2,1)S(1)}, bf16[144,256]{1,0:T(8,128)(2,1)S(1)}, u32[]{:S(2)}, u32[]{:S(2)}) %collective-permute-start.9) | collective-permute-done | bytes 73760 | tf_op jit(solution)/shard_map/ppermute | solution.py:35
  29.0 0.9 %shard_map.82 = (f32[2,64,256]{2,1,0:T(8,128)}, f32[2,64,256]{2,1,0:T(8,128)}) custom-call(f32[128,256]{1,0:T(8,128)S(1)} %get-tuple-element.38.own_corr, bf16[64,128]{1,0:T(8,128)(2,1)S(1)} %get-tuple-element.39.own_back, bf16[4,4,32,512]{3,2,1,0:T(8,128)(2,1)S(1)} %shard_map.81.basis_ref, bf16[144,256]{1,0:T(8,128)(2,1)S(1)} %collective-permute-done.8.refs_0_, ...), custom_call_target="tpu_custom_call" | custom-call | tf_op jit(solution)/shard_map/pallas_call | solution.py:235
  (11 shorter events, 0.0 us)
Async XLA Ops:
  0.6 1.7 %collective-permute-start.1 = (bf16[2,16,4,256]{3,2,1,0:T(4,128)(2,1)}, bf16[2,16,4,256]{3,2,1,0:T(4,128)(2,1)S(1)}, u32[]{:S(2)}, u32[]{:S(2)}) collective-permute-start(bf16[2,16,4,256]{3,2,1,0:T(4,128)(2,1)} %refs_0_.1), channel_id=1, source_target_pairs={{0,1},{1,0},{2,3},{3,2},{4,5},{5,4},{6,7},{7,6},{8,9},{9,8},{10,11... | collective-permute-start | bytes 196616 | tf_op jit(solution)/shard_map/ppermute | solution.py:28
  2.7 7.3 %collective-permute-start.3 = (bf16[64,256]{1,0:T(8,128)(2,1)S(1)}, bf16[64,256]{1,0:T(8,128)(2,1)S(1)}, u32[]{:S(2)}, u32[]{:S(2)}) collective-permute-start(bf16[64,256]{1,0:T(8,128)(2,1)S(1)} %get-tuple-element.30), channel_id=1, source_target_pairs={{0,4},{1,7},{2,6},{3,5},{4,0},{5,3},{6,2},{7,1},{8,12},{9,15},{10,... | collective-permute-start | bytes 98312 | tf_op jit(solution)/shard_map/ppermute | solution.py:35
  5.7 5.7 %collective-permute-start.4 = (bf16[64,256]{1,0:T(8,128)(2,1)S(1)}, bf16[64,256]{1,0:T(8,128)(2,1)S(1)}, u32[]{:S(2)}, u32[]{:S(2)}) collective-permute-start(bf16[64,256]{1,0:T(8,128)(2,1)S(1)} %get-tuple-element.31), channel_id=1, source_target_pairs={{0,8},{1,11},{2,10},{3,9},{4,12},{5,15},{6,14},{7,13},{8,0},{9,3},... | collective-permute-start | bytes 98312 | tf_op jit(solution)/shard_map/ppermute | solution.py:35
  8.3 7.1 %collective-permute-start.5 = (bf16[64,256]{1,0:T(8,128)(2,1)S(1)}, bf16[64,256]{1,0:T(8,128)(2,1)S(1)}, u32[]{:S(2)}, u32[]{:S(2)}) collective-permute-start(bf16[64,256]{1,0:T(8,128)(2,1)S(1)} %get-tuple-element.32), channel_id=1, source_target_pairs={{0,12},{1,15},{2,14},{3,13},{4,8},{5,11},{6,10},{7,9},{8,4},{9,7},... | collective-permute-start | bytes 98312 | tf_op jit(solution)/shard_map/ppermute | solution.py:35
  8.3 7.0 %collective-permute-start.2 = (bf16[72,4,256]{2,1,0:T(4,128)(2,1)S(1)}, bf16[72,4,256]{2,1,0:T(4,128)(2,1)S(1)}, u32[]{:S(2)}, u32[]{:S(2)}) collective-permute-start(bf16[72,4,256]{2,1,0:T(4,128)(2,1)S(1)} %get-tuple-element.28), channel_id=1, source_target_pairs={{0,2},{1,3},{2,0},{3,1},{4,6},{5,7},{6,4},{7,5},{8,10},{9,11},{10,... | collective-permute-start | bytes 442376 | tf_op jit(solution)/shard_map/ppermute | solution.py:28
  10.0 5.8 %copy-start = (bf16[2,16,4,256]{3,2,1,0:T(4,128)(2,1)S(1)}, bf16[2,16,4,256]{3,2,1,0:T(4,128)(2,1)}, u32[]{:S(2)}) copy-start(bf16[2,16,4,256]{3,2,1,0:T(4,128)(2,1)} %refs_1_.1) | copy-start | bytes 196612
  15.2 2.3 %collective-permute-start.7 = (bf16[72,4,256]{2,1,0:T(4,128)(2,1)S(1)}, bf16[72,4,256]{2,1,0:T(4,128)(2,1)S(1)}, u32[]{:S(2)}, u32[]{:S(2)}) collective-permute-start(bf16[72,4,256]{2,1,0:T(4,128)(2,1)S(1)} %collective-permute-done.2.far_ref), channel_id=1, source_target_pairs={{0,1},{1,0},{2,3},{3,2},{4,5},{5,4},{6,7},{7,6},{8,9},{9,8},{10,11... | collective-permute-start | bytes 442376 | tf_op jit(solution)/shard_map/ppermute | solution.py:28
  15.4 2.7 %collective-permute-start.6 = (bf16[192,256]{1,0:T(8,128)(2,1)S(1)}, bf16[192,256]{1,0:T(8,128)(2,1)S(1)}, u32[]{:S(2)}, u32[]{:S(2)}) collective-permute-start(bf16[192,256]{1,0:T(8,128)(2,1)S(1)} %constant_dynamic-update-slice_fusion.mine_ref), channel_id=1, source_target_pairs={{0,1},{1,0},{2,3},{3,2},{4,5},{5,4},{6,7},{7,6},{8,9},{9,8},{10,11... | collective-permute-start | bytes 294920 | tf_op jit(solution)/shard_map/ppermute | solution.py:28
  15.8 1.3 %collective-permute-start = (bf16[2,16,4,256]{3,2,1,0:T(4,128)(2,1)S(1)}, bf16[2,16,4,256]{3,2,1,0:T(4,128)(2,1)S(1)}, u32[]{:S(2)}, u32[]{:S(2)}) collective-permute-start(bf16[2,16,4,256]{3,2,1,0:T(4,128)(2,1)S(1)} %copy-done), channel_id=1, source_target_pairs={{0,1},{1,0},{2,3},{3,2},{4,5},{5,4},{6,7},{7,6},{8,9},{9,8},{10,11... | collective-permute-start | bytes 196616 | tf_op jit(solution)/shard_map/ppermute | solution.py:28
  18.7 7.1 %collective-permute-start.10 = (bf16[144,256]{1,0:T(8,128)(2,1)S(1)}, bf16[144,256]{1,0:T(8,128)(2,1)S(1)}, u32[]{:S(2)}, u32[]{:S(2)}) collective-permute-start(bf16[144,256]{1,0:T(8,128)(2,1)S(1)} %get-tuple-element.42), channel_id=1, source_target_pairs={{0,12},{1,13},{2,14},{3,15},{4,8},{5,9},{6,10},{7,11},{8,4},{9,5},... | collective-permute-start | bytes 221192 | tf_op jit(solution)/shard_map/ppermute | solution.py:35
  22.2 6.1 %collective-permute-start.8 = (bf16[144,256]{1,0:T(8,128)(2,1)S(1)}, bf16[144,256]{1,0:T(8,128)(2,1)S(1)}, u32[]{:S(2)}, u32[]{:S(2)}) collective-permute-start(bf16[144,256]{1,0:T(8,128)(2,1)S(1)} %get-tuple-element.40), channel_id=1, source_target_pairs={{0,4},{1,5},{2,6},{3,7},{4,0},{5,1},{6,2},{7,3},{8,12},{9,13},{10,... | collective-permute-start | bytes 221192 | tf_op jit(solution)/shard_map/ppermute | solution.py:35
  22.2 6.8 %collective-permute-start.9 = (bf16[144,256]{1,0:T(8,128)(2,1)S(1)}, bf16[144,256]{1,0:T(8,128)(2,1)S(1)}, u32[]{:S(2)}, u32[]{:S(2)}) collective-permute-start(bf16[144,256]{1,0:T(8,128)(2,1)S(1)} %get-tuple-element.41), channel_id=1, source_target_pairs={{0,8},{1,9},{2,10},{3,11},{4,12},{5,13},{6,14},{7,15},{8,0},{9,1},... | collective-permute-start | bytes 221192 | tf_op jit(solution)/shard_map/ppermute | solution.py:35
